TPU v7x, 256 devices: a whole 4x4x8 slice. The times are simulated.
256 devices in a mesh: layer: 4 (over x), row: 8 (over y, core), col: 8 (over z).
Axes of the slice: x: 4, y: 4, z: 8, core: 2. Of those that a mesh axis runs over, the one named last changes fastest.
Arguments:
- cols: int32 [512, 16], P(('row', 'col'), 'layer'), may hold values from -1 to 511, as said below
- vals: bfloat16 [512, 16, 256, 256], P(('row', 'col'), 'layer'), as said below
- outcols: int32 [512, 4], P(('row', 'col')), may hold values from -1 to 511, as said below
Outputs:
- purified: bfloat16 [512, 4, 256, 256], P(('row', 'col'), 'layer')
Inputs may be any that keep to these rules, and one draw needn't show every extreme that they name: `cols`: slots 4 * l to 4 * l + 3 of block row i hold distinct block columns k with k mod 4 = l and |k - i| <= 6, or -1. Column i is always listed in row i, and k is listed in row i exactly when i is listed in row k. vals[i, s] is block (i, cols[i, s]) of a symmetric matrix: the block listed at (k, i) is the transpose of the one at (i, k). Slots holding -1 hold zeros. `outcols`: block row i lists distinct block columns j with i <= j <= i + 12, always i itself, or -1.
All inputs are finite; a program needn't handle non-finite values.
Results may differ from a plain program's by a relative error of at most 0.0085.
Values may be sent and summed in bfloat16 or wider, within the bound.
No kernel may reach another device: no remote copies, remote signals or barrier semaphores. Data moves between devices by JAX's collectives and lax.ppermute only.
A program may use at most 64 MiB of HBM per device.

v0:
```python
import jax
import jax.numpy as jnp
from jax import lax
from jax.sharding import PartitionSpec as P

W = 6


def passed_along(value, axis, by):
    peers = lax.axis_size(axis)
    pairs = [(i, i + by) for i in range(peers) if 0 <= i + by < peers]
    return lax.ppermute(value, axis, pairs)


def per_device(cols, vals, outcols):
    rows = vals.shape[0]
    need = 2 * W
    hops = -(-need // rows)
    blocks_list = [vals]
    column_list = [cols]
    for hop in range(1, hops + 1):
        count = min(rows, need - (hop - 1) * rows)
        got_blocks, got_cols = passed_along((vals[:count], cols[:count]), ("row", "col"), -hop)
        blocks_list.append(got_blocks)
        column_list.append(got_cols)
    extended = jnp.concatenate(blocks_list, axis=0)
    extended_cols = jnp.concatenate(column_list, axis=0)
    offset_rows = lax.axis_index(("row", "col")) * rows

    def one_row(inputs):
        left, left_cols, targets = inputs
        where = jnp.clip(targets - offset_rows, 0, extended_cols.shape[0] - 1)
        right = extended[where]
        right_cols = extended_cols[where]
        hits = (
            (left_cols[None, :, None] == right_cols[:, None, :]) & (left_cols[None, :, None] >= 0)
        ).astype(jnp.bfloat16)
        moved = jnp.einsum(
            "ost,otab->osab", hits, right, preferred_element_type=jnp.float32
        ).astype(jnp.bfloat16)
        product = jnp.einsum("sab,oscb->oac", left, moved, preferred_element_type=jnp.float32)
        owned = (left_cols[None, :] == targets[:, None]).astype(jnp.bfloat16)
        twice = 2.0 * jnp.einsum("os,sab->oab", owned, left, preferred_element_type=jnp.float32)
        return jnp.where(targets[:, None, None] >= 0, twice - product, jnp.float32(0.0))

    partials = lax.map(one_row, (vals, cols, outcols))
    total = lax.psum(partials.astype(jnp.bfloat16), "layer").astype(jnp.float32)
    share = outcols.shape[1] // lax.axis_size("layer")
    mine = lax.dynamic_slice_in_dim(total, lax.axis_index("layer") * share, share, 1)
    return mine.astype(jnp.bfloat16)


def solution(mesh):
    in_specs = (
        P(("row", "col"), "layer"),
        P(("row", "col"), "layer", None, None),
        P(("row", "col"), None),
    )
    out_specs = P(("row", "col"), "layer", None, None)
    return jax.shard_map(
        per_device, mesh=mesh, in_specs=in_specs, out_specs=out_specs, check_vma=False
    )
```

profile of v0, /device:TPU:1, one launch (start us, length us, event | category | flops | bytes accessed | tf_op | source)
XLA Modules:
  0.0 402.7 jit_solution(4357979554235664735)
XLA Ops:
  6.5 9.0 %collective-permute-start.2 = (bf16[8,4,256,256]{3,2,1,0:T(8,128)(2,1)}, bf16[8,4,256,256]{3,2,1,0:T(8,128)(2,1)}, u32[]{:S(2)}, u32[]{:S(2)}) collective-permute-start(bf16[8,4,256,256]{3,2,1,0:T(8,128)(2,1)} %param.6), channel_id=1, source_target_pairs={{1,0},{2,1},{3,2},{4,3},{5,4},{6,5},{7,6},{8,7},{9,8},{10,9},{11,1... | collective-permute-start | bytes 12582920 | tf_op jit(solution)/shard_map/ppermute | solution.py:12
  15.5 3.1 slice.7
  18.7 3.3 collective-permute-start.3
  22.0 2.9 collective-permute-start
  25.0 1.9 collective-permute-start.1
  27.1 165.7 %collective-permute-done.1 = s32[4,4]{0,1:T(4,128)S(1)} collective-permute-done((s32[4,4]{0,1:T(4,128)S(1)}, s32[4,4]{0,1:T(4,128)S(1)}, u32[]{:S(2)}, u32[]{:S(2)}) %collective-permute-start.1) | collective-permute-done | bytes 96 | tf_op jit(solution)/shard_map/ppermute | solution.py:12
  193.0 8.8 %pad_maximum_fusion = bf16[20,4,256,256]{3,2,1,0:T(8,128)(2,1)} fusion(bf16[4,4,256,256]{3,2,1,0:T(8,128)(2,1)S(1)} %collective-permute-done.3, bf16[8,4,256,256]{3,2,1,0:T(8,128)(2,1)} %collective-permute-done.2, bf16[8,4,256,256]{3,2,1,0:T(8,128)(2,1)} %param.6), kind=kLoop, calls=%fused_computation.35 | loop fusion | flops 10485760 | bytes 20971520 | tf_op jit(solution)/shard_map/concatenate | solution.py:26
  201.8 90.1 %while.10 = (s32[]{:T(128)}, bf16[8,4,256,256]{3,2,1,0:T(8,128)(2,1)}, s32[8,4]{1,0:T(8,128)S(1)}, s32[8,4]{1,0:T(8,128)S(1)}, bf16[8,4,256,256]{3,2,1,0:T(8,128...) while((s32[]{:T(128)}, bf16[8,4,256,256]{3,2,1,0:T(8,128)(2,1)}, ...), condition=%wide.region_1.2_spmd, body=%wide.region_0.1_spmd.sunk | while | flops 548144256 | bytes 19403772 | solution.py:46
  201.8 4.7 %gather_fusion = bf16[4,4,256,256]{3,2,1,0:T(8,128)(2,1)S(1)} fusion(bf16[20,4,256,256]{3,2,1,0:T(8,128)(2,1)} %get-tuple-element.168, s32[1024]{0:T(1024)S(1)} %pad_clamp_fusion.2), kind=kCustom, calls=%fused_computation.1.clone.1 | custom fusion | bytes 4194320 | tf_op jit(solution)/shard_map/while/body/eval_jaxpr/gather | solution.py:33
  207.1 1.8 fusion.37
  208.8 1.1 constant_dynamic-slice_fusion.4
  212.2 0.9 copy_dynamic-update-slice_fusion.2
  213.1 4.7 %gather_fusion = bf16[4,4,256,256]{3,2,1,0:T(8,128)(2,1)S(1)} fusion(bf16[20,4,256,256]{3,2,1,0:T(8,128)(2,1)} %get-tuple-element.168, s32[1024]{0:T(1024)S(1)} %pad_clamp_fusion.2), kind=kCustom, calls=%fused_computation.1.clone.1 | custom fusion | bytes 4194320 | tf_op jit(solution)/shard_map/while/body/eval_jaxpr/gather | solution.py:33
  218.3 1.8 fusion.37
  220.1 1.1 constant_dynamic-slice_fusion.4
  221.6 0.8 fusion.38
  223.4 0.9 copy_dynamic-update-slice_fusion.2
  224.3 4.7 %gather_fusion = bf16[4,4,256,256]{3,2,1,0:T(8,128)(2,1)S(1)} fusion(bf16[20,4,256,256]{3,2,1,0:T(8,128)(2,1)} %get-tuple-element.168, s32[1024]{0:T(1024)S(1)} %pad_clamp_fusion.2), kind=kCustom, calls=%fused_computation.1.clone.1 | custom fusion | bytes 4194320 | tf_op jit(solution)/shard_map/while/body/eval_jaxpr/gather | solution.py:33
  229.6 1.8 fusion.37
  231.3 1.1 constant_dynamic-slice_fusion.4
  232.8 0.8 fusion.38
  234.7 0.9 copy_dynamic-update-slice_fusion.2
  235.6 4.7 %gather_fusion = bf16[4,4,256,256]{3,2,1,0:T(8,128)(2,1)S(1)} fusion(bf16[20,4,256,256]{3,2,1,0:T(8,128)(2,1)} %get-tuple-element.168, s32[1024]{0:T(1024)S(1)} %pad_clamp_fusion.2), kind=kCustom, calls=%fused_computation.1.clone.1 | custom fusion | bytes 4194320 | tf_op jit(solution)/shard_map/while/body/eval_jaxpr/gather | solution.py:33
  240.8 1.8 fusion.37
  242.6 1.1 constant_dynamic-slice_fusion.4
  244.1 0.8 fusion.38
  245.9 0.9 copy_dynamic-update-slice_fusion.2
  246.9 4.7 %gather_fusion = bf16[4,4,256,256]{3,2,1,0:T(8,128)(2,1)S(1)} fusion(bf16[20,4,256,256]{3,2,1,0:T(8,128)(2,1)} %get-tuple-element.168, s32[1024]{0:T(1024)S(1)} %pad_clamp_fusion.2), kind=kCustom, calls=%fused_computation.1.clone.1 | custom fusion | bytes 4194320 | tf_op jit(solution)/shard_map/while/body/eval_jaxpr/gather | solution.py:33
  252.1 1.8 fusion.37
  253.9 1.1 constant_dynamic-slice_fusion.4
  255.4 0.8 fusion.38
  257.2 0.9 copy_dynamic-update-slice_fusion.2
  258.1 4.7 %gather_fusion = bf16[4,4,256,256]{3,2,1,0:T(8,128)(2,1)S(1)} fusion(bf16[20,4,256,256]{3,2,1,0:T(8,128)(2,1)} %get-tuple-element.168, s32[1024]{0:T(1024)S(1)} %pad_clamp_fusion.2), kind=kCustom, calls=%fused_computation.1.clone.1 | custom fusion | bytes 4194320 | tf_op jit(solution)/shard_map/while/body/eval_jaxpr/gather | solution.py:33
  263.4 1.8 fusion.37
  265.1 1.1 constant_dynamic-slice_fusion.4
  266.6 0.8 fusion.38
  268.5 0.9 copy_dynamic-update-slice_fusion.2
  269.4 4.7 %gather_fusion = bf16[4,4,256,256]{3,2,1,0:T(8,128)(2,1)S(1)} fusion(bf16[20,4,256,256]{3,2,1,0:T(8,128)(2,1)} %get-tuple-element.168, s32[1024]{0:T(1024)S(1)} %pad_clamp_fusion.2), kind=kCustom, calls=%fused_computation.1.clone.1 | custom fusion | bytes 4194320 | tf_op jit(solution)/shard_map/while/body/eval_jaxpr/gather | solution.py:33
  274.6 1.8 fusion.37
  276.4 1.1 constant_dynamic-slice_fusion.4
  279.8 0.9 copy_dynamic-update-slice_fusion.2
  280.7 4.7 %gather_fusion = bf16[4,4,256,256]{3,2,1,0:T(8,128)(2,1)S(1)} fusion(bf16[20,4,256,256]{3,2,1,0:T(8,128)(2,1)} %get-tuple-element.168, s32[1024]{0:T(1024)S(1)} %pad_clamp_fusion.2), kind=kCustom, calls=%fused_computation.1.clone.1 | custom fusion | bytes 4194320 | tf_op jit(solution)/shard_map/while/body/eval_jaxpr/gather | solution.py:33
  285.9 1.8 fusion.37
  287.7 1.1 constant_dynamic-slice_fusion.4
  289.2 0.8 fusion.38
  291.0 0.8 copy_dynamic-update-slice_fusion.2
  291.9 101.7 %all-reduce.2.cloned.1.call-done = bf16[8,4,256,256]{3,2,1,0:T(8,128)(2,1)} async-done(((bf16[8,4,256,256]{3,2,1,0:T(8,128)(2,1)}), bf16[8,4,256,256]{3,2,1,0:T(8,128)(2,1)}) %all-reduce.2.cloned.1.call-update) | async-done | bytes 4194320 | tf_op jit(solution)/shard_map/psum | solution.py:47
  393.6 2.3 convert_convert_fusion
  (72 shorter events, 18.4 us)
Async XLA Ops:
  6.5 15.5 %copy-start = (s32[8,4]{0,1:T(4,128)S(1)}, s32[8,4]{0,1:T(4,128)}, u32[]{:S(2)}) copy-start(s32[8,4]{0,1:T(4,128)} %param.5) | copy-start | bytes 388
  6.5 20.5 %copy-start.1 = (s32[8,4]{0,1:T(4,128)S(1)}, s32[8,4]{0,1:T(4,128)}, u32[]{:S(2)}) copy-start(s32[8,4]{0,1:T(4,128)} %param.7) | copy-start | bytes 388
  6.5 387.0 %all-reduce.2.cloned.1.call-start = ((), (), s32[]{:S(2)}) async-start(), calls=%async_computation | async-start | bytes 8388608 | tf_op jit(solution)/shard_map/psum | solution.py:47
  6.5 186.4 %collective-permute-start.2 = (bf16[8,4,256,256]{3,2,1,0:T(8,128)(2,1)}, bf16[8,4,256,256]{3,2,1,0:T(8,128)(2,1)}, u32[]{:S(2)}, u32[]{:S(2)}) collective-permute-start(bf16[8,4,256,256]{3,2,1,0:T(8,128)(2,1)} %param.6), channel_id=1, source_target_pairs={{1,0},{2,1},{3,2},{4,3},{5,4},{6,5},{7,6},{8,7},{9,8},{10,9},{11,1... | collective-permute-start | bytes 12582920 | tf_op jit(solution)/shard_map/ppermute | solution.py:12
  18.7 174.3 %collective-permute-start.3 = (bf16[4,4,256,256]{3,2,1,0:T(8,128)(2,1)}, bf16[4,4,256,256]{3,2,1,0:T(8,128)(2,1)S(1)}, u32[]{:S(2)}, u32[]{:S(2)}) collective-permute-start(bf16[4,4,256,256]{3,2,1,0:T(8,128)(2,1)} %slice.7), channel_id=1, source_target_pairs={{2,0},{3,1},{4,2},{5,3},{6,4},{7,5},{8,6},{9,7},{10,8},{11,9},{12,... | collective-permute-start | bytes 6291464 | tf_op jit(solution)/shard_map/ppermute | solution.py:12
  22.0 170.8 %collective-permute-start = (s32[8,4]{0,1:T(4,128)S(1)}, s32[8,4]{0,1:T(4,128)S(1)}, u32[]{:S(2)}, u32[]{:S(2)}) collective-permute-start(s32[8,4]{0,1:T(4,128)S(1)} %copy-done), channel_id=1, source_target_pairs={{1,0},{2,1},{3,2},{4,3},{5,4},{6,5},{7,6},{8,7},{9,8},{10,9},{11,1... | collective-permute-start | bytes 392 | tf_op jit(solution)/shard_map/ppermute | solution.py:12
  25.0 167.8 %collective-permute-start.1 = (s32[4,4]{0,1:T(4,128)S(1)}, s32[4,4]{0,1:T(4,128)S(1)}, u32[]{:S(2)}, u32[]{:S(2)}) collective-permute-start(s32[4,4]{0,1:T(4,128)S(1)} %bitcast.54), channel_id=1, source_target_pairs={{2,0},{3,1},{4,2},{5,3},{6,4},{7,5},{8,6},{9,7},{10,8},{11,9},{12,... | collective-permute-start | bytes 200 | tf_op jit(solution)/shard_map/ppermute | solution.py:12
Sparse Core Ops, SparseCore 0:
  292.0 101.5 all-reduce.1
where the time goes:
time: 404 us; the launch traced here: 403 us
  waiting for transfers between devices  267 us (66%)
  local copies, waits for them, and re-layouts  67.3 us (17%)
  matrix products  25.5 us (6%)
  starting transfers between devices  17.2 us (4%)
  between operations  13.5 us (3%)
  other arithmetic  11.4 us (3%)
    ppermute x4, waiting for transfers between devices, passed_along(): return lax.ppermute(value, axis, pairs)  166 us
    psum x1, waiting for transfers between devices, per_device(): total = lax.psum(partials.astype(jnp.bfloat16), 'layer').astype(jnp.float32)  102 us
    gather x8, local copies, waits for them, and re-layouts, one_row(): right = extended[where]  37.3 us
    ppermute x4, starting transfers between devices, passed_along(): return lax.ppermute(value, axis, pairs)  17.2 us
    dot_general x8, matrix products, one_row(): jnp.einsum('ost,otab->osab', hits, right, preferred_element_type=jnp.floa...  14.1 us
    dynamic_slice x16, local copies, waits for them, and re-layouts, per_device(): partials = lax.map(one_row, (vals, cols, outcols))  11.9 us
    concatenate x1, other arithmetic, per_device(): extended = jnp.concatenate(blocks_list, axis=0)  8.8 us
  transfers between devices with their start and end apart: 5, of which 2 were waited for; matrix products, arithmetic and copies ran while one was open for 1% of the time, Pallas kernels for 0%

commit v1 on v0

--- a/solution.py
+++ b/solution.py
@@ -44,7 +44,9 @@
         return jnp.where(targets[:, None, None] >= 0, twice - product, jnp.float32(0.0))
 
     partials = lax.map(one_row, (vals, cols, outcols))
-    total = lax.psum(partials.astype(jnp.bfloat16), "layer").astype(jnp.float32)
+    total = jnp.sum(lax.all_gather(partials.astype(jnp.bfloat16), "layer"), axis=0).astype(
+        jnp.float32
+    )
     share = outcols.shape[1] // lax.axis_size("layer")
     mine = lax.dynamic_slice_in_dim(total, lax.axis_index("layer") * share, share, 1)
     return mine.astype(jnp.bfloat16)

time: 404 us -> 474 us (1.17)
  waiting for transfers between devices: 267 us -> 326 us
  other arithmetic: 11.4 us -> 23 us
    all_gather x0 -> x1, waiting for transfers between devices: none -> 160 us  [per_device(): lax.all_gather(partials.astype(jnp.bfloat16), 'layer')]
    psum x1 -> x0, waiting for transfers between devices: 102 us -> none  [per_device(): total = lax.psum(partials.astype(jnp.bfloat16), 'layer').astype(jnp.float32)]
    reduce_sum x0 -> x1, other arithmetic: none -> 11.7 us  [per_device(): jnp.sum(lax.all_gather(partials.astype(jnp.bfloat16), 'layer'), axis=0)]
where the time goes in v1:
time: 474 us; the launch traced here: 473 us
  waiting for transfers between devices  326 us (69%)
  local copies, waits for them, and re-layouts  67.2 us (14%)
  matrix products  25.5 us (5%)
  other arithmetic  23 us (5%)
  starting transfers between devices  17.2 us (4%)
  between operations  13.5 us (3%)
    ppermute x4, waiting for transfers between devices, passed_along(): return lax.ppermute(value, axis, pairs)  166 us
    all_gather x1, waiting for transfers between devices, per_device(): lax.all_gather(partials.astype(jnp.bfloat16), 'layer')  160 us
    gather x8, local copies, waits for them, and re-layouts, one_row(): right = extended[where]  37.3 us
    ppermute x4, starting transfers between devices, passed_along(): return lax.ppermute(value, axis, pairs)  17.2 us
    dot_general x8, matrix products, one_row(): jnp.einsum('ost,otab->osab', hits, right, preferred_element_type=jnp.floa...  14.1 us
    dynamic_slice x16, local copies, waits for them, and re-layouts, per_device(): partials = lax.map(one_row, (vals, cols, outcols))  11.9 us
    reduce_sum x1, other arithmetic, per_device(): jnp.sum(lax.all_gather(partials.astype(jnp.bfloat16), 'layer'), axis=0)  11.7 us
  transfers between devices with their start and end apart: 5, of which 2 were waited for; matrix products, arithmetic and copies ran while one was open for 1% of the time, Pallas kernels for 0%

profile of v1, /device:TPU:1, one launch (start us, length us, event | category | flops | bytes accessed | tf_op | source)
XLA Modules:
  0.0 473.0 jit_solution(13063474419698054895)
XLA Ops:
  6.5 9.0 %collective-permute-start.2 = (bf16[8,4,256,256]{3,2,1,0:T(8,128)(2,1)}, bf16[8,4,256,256]{3,2,1,0:T(8,128)(2,1)}, u32[]{:S(2)}, u32[]{:S(2)}) collective-permute-start(bf16[8,4,256,256]{3,2,1,0:T(8,128)(2,1)} %param.6), channel_id=1, source_target_pairs={{1,0},{2,1},{3,2},{4,3},{5,4},{6,5},{7,6},{8,7},{9,8},{10,9},{11,1... | collective-permute-start | bytes 12582920 | tf_op jit(solution)/shard_map/ppermute | solution.py:12
  15.5 3.1 slice.7
  18.7 3.3 collective-permute-start.3
  22.0 2.9 collective-permute-start
  24.9 1.9 collective-permute-start.1
  27.0 165.8 %collective-permute-done.1 = s32[4,4]{0,1:T(4,128)S(1)} collective-permute-done((s32[4,4]{0,1:T(4,128)S(1)}, s32[4,4]{0,1:T(4,128)S(1)}, u32[]{:S(2)}, u32[]{:S(2)}) %collective-permute-start.1) | collective-permute-done | bytes 96 | tf_op jit(solution)/shard_map/ppermute | solution.py:12
  193.0 8.7 %pad_maximum_fusion = bf16[20,4,256,256]{3,2,1,0:T(8,128)(2,1)} fusion(bf16[4,4,256,256]{3,2,1,0:T(8,128)(2,1)S(1)} %collective-permute-done.3, bf16[8,4,256,256]{3,2,1,0:T(8,128)(2,1)} %collective-permute-done.2, bf16[8,4,256,256]{3,2,1,0:T(8,128)(2,1)} %param.6), kind=kLoop, calls=%fused_computation.35 | loop fusion | flops 10485760 | bytes 20971520 | tf_op jit(solution)/shard_map/concatenate | solution.py:26
  201.7 90.0 %while.10 = (s32[]{:T(128)}, bf16[8,4,256,256]{3,2,1,0:T(8,128)(2,1)}, s32[8,4]{1,0:T(8,128)S(1)}, s32[8,4]{1,0:T(8,128)S(1)}, bf16[8,4,256,256]{3,2,1,0:T(8,128...) while((s32[]{:T(128)}, bf16[8,4,256,256]{3,2,1,0:T(8,128)(2,1)}, ...), condition=%wide.region_1.2_spmd, body=%wide.region_0.1_spmd.sunk | while | flops 548144256 | bytes 19403772 | solution.py:46
  201.7 4.7 gather_fusion
  207.0 1.8 fusion.37
  208.7 1.1 constant_dynamic-slice_fusion.4
  212.1 0.9 copy_dynamic-update-slice_fusion.2
  213.0 4.7 gather_fusion
  218.2 1.8 fusion.37
  220.0 1.1 constant_dynamic-slice_fusion.4
  221.5 0.8 fusion.38
  223.3 0.9 copy_dynamic-update-slice_fusion.2
  224.2 4.7 gather_fusion
  229.5 1.8 fusion.37
  231.2 1.1 constant_dynamic-slice_fusion.4
  232.7 0.8 fusion.38
  234.6 0.9 copy_dynamic-update-slice_fusion.2
  235.5 4.7 gather_fusion
  240.7 1.8 fusion.37
  242.5 1.1 constant_dynamic-slice_fusion.4
  245.8 0.9 copy_dynamic-update-slice_fusion.2
  246.8 4.7 gather_fusion
  252.0 1.8 fusion.37
  253.8 1.1 constant_dynamic-slice_fusion.4
  255.3 0.8 fusion.38
  257.1 0.9 copy_dynamic-update-slice_fusion.2
  258.0 4.7 gather_fusion
  263.2 1.8 fusion.37
  265.0 1.1 constant_dynamic-slice_fusion.4
  268.4 0.9 copy_dynamic-update-slice_fusion.2
  269.3 4.7 gather_fusion
  274.5 1.8 fusion.37
  276.3 1.1 constant_dynamic-slice_fusion.4
  277.8 0.8 fusion.38
  279.6 0.9 copy_dynamic-update-slice_fusion.2
  280.5 4.7 gather_fusion
  285.7 1.8 fusion.37
  287.5 1.1 constant_dynamic-slice_fusion.4
  289.0 0.8 fusion.38
  290.9 0.9 copy_dynamic-update-slice_fusion.2
  291.8 160.4 %all-gather.3.cloned.1.call-done = bf16[32,4,256,256]{3,2,1,0:T(8,128)(2,1)} async-done(((bf16[8,4,256,256]{3,2,1,0:T(8,128)(2,1)}), bf16[32,4,256,256]{3,2,1,0:T(8,128)(2,1)}) %all-gather.3.cloned.1.call-update) | async-done | bytes 16777232 | tf_op jit(solution)/shard_map/all_gather | solution.py:47
  452.2 11.7 %reduce_sum.12 = bf16[8,4,256,256]{3,2,1,0:T(8,128)(2,1)} reduce(bf16[4,8,4,256,256]{4,3,2,1,0:T(8,128)(2,1)} %bitcast.54, bf16[]{:T(256)} %constant.44.clone.1), dimensions={0}, to_apply=%region_2.3 | reduce | flops 6291456 | bytes 20971522 | tf_op jit(solution)/shard_map/reduce_sum | solution.py:47
  463.9 2.3 convert_convert_fusion
  (73 shorter events, 19.1 us)
Async XLA Ops:
  6.5 15.5 %copy-start = (s32[8,4]{0,1:T(4,128)S(1)}, s32[8,4]{0,1:T(4,128)}, u32[]{:S(2)}) copy-start(s32[8,4]{0,1:T(4,128)} %param.5) | copy-start | bytes 388
  6.5 20.4 %copy-start.1 = (s32[8,4]{0,1:T(4,128)S(1)}, s32[8,4]{0,1:T(4,128)}, u32[]{:S(2)}) copy-start(s32[8,4]{0,1:T(4,128)} %param.7) | copy-start | bytes 388
  6.5 445.6 %all-gather.3.cloned.1.call-start = ((), (), s32[]{:S(2)}) async-start(), calls=%async_computation | async-start | bytes 20971520 | tf_op jit(solution)/shard_map/all_gather | solution.py:47
  6.5 186.4 %collective-permute-start.2 = (bf16[8,4,256,256]{3,2,1,0:T(8,128)(2,1)}, bf16[8,4,256,256]{3,2,1,0:T(8,128)(2,1)}, u32[]{:S(2)}, u32[]{:S(2)}) collective-permute-start(bf16[8,4,256,256]{3,2,1,0:T(8,128)(2,1)} %param.6), channel_id=1, source_target_pairs={{1,0},{2,1},{3,2},{4,3},{5,4},{6,5},{7,6},{8,7},{9,8},{10,9},{11,1... | collective-permute-start | bytes 12582920 | tf_op jit(solution)/shard_map/ppermute | solution.py:12
  18.7 174.3 %collective-permute-start.3 = (bf16[4,4,256,256]{3,2,1,0:T(8,128)(2,1)}, bf16[4,4,256,256]{3,2,1,0:T(8,128)(2,1)S(1)}, u32[]{:S(2)}, u32[]{:S(2)}) collective-permute-start(bf16[4,4,256,256]{3,2,1,0:T(8,128)(2,1)} %slice.7), channel_id=1, source_target_pairs={{2,0},{3,1},{4,2},{5,3},{6,4},{7,5},{8,6},{9,7},{10,8},{11,9},{12,... | collective-permute-start | bytes 6291464 | tf_op jit(solution)/shard_map/ppermute | solution.py:12
  22.0 170.8 %collective-permute-start = (s32[8,4]{0,1:T(4,128)S(1)}, s32[8,4]{0,1:T(4,128)S(1)}, u32[]{:S(2)}, u32[]{:S(2)}) collective-permute-start(s32[8,4]{0,1:T(4,128)S(1)} %copy-done), channel_id=1, source_target_pairs={{1,0},{2,1},{3,2},{4,3},{5,4},{6,5},{7,6},{8,7},{9,8},{10,9},{11,1... | collective-permute-start | bytes 392 | tf_op jit(solution)/shard_map/ppermute | solution.py:12
  24.9 167.9 %collective-permute-start.1 = (s32[4,4]{0,1:T(4,128)S(1)}, s32[4,4]{0,1:T(4,128)S(1)}, u32[]{:S(2)}, u32[]{:S(2)}) collective-permute-start(s32[4,4]{0,1:T(4,128)S(1)} %bitcast.56), channel_id=1, source_target_pairs={{2,0},{3,1},{4,2},{5,3},{6,4},{7,5},{8,6},{9,7},{10,8},{11,9},{12,... | collective-permute-start | bytes 200 | tf_op jit(solution)/shard_map/ppermute | solution.py:12
Sparse Core Ops, SparseCore 0:
  291.9 160.2 all-gather.2
